TPU v7x, 256 devices: a whole 4x4x8 slice. The times are simulated.
256 devices in a mesh: fsdp: 32 (over z, y_hi, core), dp: 8 (over y_lo, x).
Axes of the slice: x: 4, y: 4 (y_hi: 2, y_lo: 2; y = y_hi * 2 + y_lo), z: 8, core: 2. Of those that a mesh axis runs over, the one named last changes fastest.
Arguments:
- features: bfloat16 [256, 16, 16, 640], P(('fsdp', 'dp')), may hold values from -100 to 100
- weight: bfloat16 [640, 5760], P('fsdp'), may hold values from -0.078125 to 0.078125
- group_norm_gain: float32 [640], replicated, may hold values from 0.1 to 1.9
- group_norm_shift: float32 [640], replicated, may hold values from -3 to 3
- conv_bias: float32 [640], replicated, may hold values from -3 to 3
- cotangent: bfloat16 [256, 16, 16, 640], P(('fsdp', 'dp')), may hold values from -6 to 6
Outputs:
- output: bfloat16 [256, 16, 16, 640], P(('fsdp', 'dp'))
- feature_gradient: bfloat16 [256, 16, 16, 640], P(('fsdp', 'dp'))
- weight_grad: float32 [640, 5760], P('fsdp')
- gain_gradient: float32 [640], replicated
- shift_grad: float32 [640], replicated
- bias_grad: float32 [640], replicated
All inputs are finite; a program needn't handle non-finite values.
Results may differ from a plain program's by a relative error of at most 0.0044.
Values may be sent and summed in bfloat16 or wider, within the bound.
A program may use at most 128 MiB of HBM per device.

v0:
```python
import jax
import jax.numpy as jnp
from jax import lax
from jax.sharding import PartitionSpec as P

GSIZE = 40


epsilon = 1e-05


def group_average(values):
    leading = values.shape[0]
    grouped = jnp.sum(values.reshape(leading, -1, GSIZE), axis=2)
    return jnp.repeat(grouped, GSIZE, axis=1)


def apply_group_norm(features):
    widened = features.astype(jnp.float32)
    entry_count = features.shape[1] * features.shape[2] * GSIZE
    average = group_average(jnp.sum(widened, axis=(1, 2))) / entry_count
    centred = widened - average[:, None, None, :]
    spread = group_average(jnp.sum(centred * centred, axis=(1, 2))) / entry_count
    inverse_deviation = lax.rsqrt(spread + epsilon)
    return (centred * inverse_deviation[:, None, None, :], inverse_deviation, entry_count)


def spatial_pad(values):
    return jnp.pad(values, ((0, 0), (1, 1), (1, 1), (0, 0)))


def tap_window(padded, tap_index, side_len, flipped):
    row_off, col_off = divmod(tap_index, 3)
    if flipped:
        row_off, col_off = (2 - row_off, 2 - col_off)
    return padded[:, row_off : row_off + side_len, col_off : col_off + side_len, :]


def local(features, weight, group_norm_gain, group_norm_shift, conv_bias, cotangent):
    local_images = features.shape[0]
    side_len = features.shape[1]
    width_in = features.shape[3]
    width_out = cotangent.shape[3]
    images = local_images * lax.axis_size("fsdp") * lax.axis_size("dp")
    normalized_input, inverse_deviation, entry_count = apply_group_norm(features)
    preactivation = normalized_input * group_norm_gain + group_norm_shift
    hidden = jax.nn.silu(preactivation).astype(jnp.bfloat16)
    hidden_pad = spatial_pad(hidden)
    grad_pad = spatial_pad(cotangent)
    full_weight = lax.all_gather(weight, "fsdp", axis=0, tiled=True)
    conv_out = jnp.zeros((local_images, side_len, side_len, width_out), jnp.float32)
    for tap_index in range(9):
        conv_out = conv_out + jnp.einsum(
            "nijc,co->nijo",
            tap_window(hidden_pad, tap_index, side_len, False),
            full_weight[:, tap_index * width_out : (tap_index + 1) * width_out],
            preferred_element_type=jnp.float32,
        )
    output = (conv_out + conv_bias).astype(jnp.bfloat16)
    back_weight = lax.all_gather(weight, "fsdp", axis=0, tiled=True)
    grad_hidden = jnp.zeros((local_images, side_len, side_len, width_in), jnp.float32)
    for tap_index in range(9):
        grad_hidden = grad_hidden + jnp.einsum(
            "nijo,co->nijc",
            tap_window(grad_pad, tap_index, side_len, True),
            back_weight[:, tap_index * width_out : (tap_index + 1) * width_out],
            preferred_element_type=jnp.float32,
        )
    columns = []
    for tap_index in range(9):
        columns.append(
            jnp.einsum(
                "nijc,nijo->co",
                tap_window(hidden_pad, tap_index, side_len, False),
                cotangent,
                preferred_element_type=jnp.float32,
            )
        )
    local_term = jnp.concatenate(columns, axis=1)
    weight_sum = lax.psum_scatter(local_term, "fsdp", scatter_dimension=0, tiled=True)
    weight_total = lax.psum(weight_sum, "dp")
    weight_grad = weight_total / images
    sigmoid = jax.nn.sigmoid(preactivation)
    preactivation_gradient = grad_hidden * sigmoid * (1.0 + preactivation * (1.0 - sigmoid))
    norm_gradient = preactivation_gradient * group_norm_gain
    first_moment = group_average(jnp.sum(norm_gradient, axis=(1, 2))) / entry_count
    second_moment = (
        group_average(jnp.sum(norm_gradient * normalized_input, axis=(1, 2))) / entry_count
    )
    feature_gradient = (
        (
            norm_gradient
            - first_moment[:, None, None, :]
            - normalized_input * second_moment[:, None, None, :]
        )
        * inverse_deviation[:, None, None, :]
    ).astype(jnp.bfloat16)
    gain_product = jnp.sum(preactivation_gradient * normalized_input, axis=(0, 1, 2))
    shift_term = jnp.sum(preactivation_gradient, axis=(0, 1, 2))
    bias_term = jnp.sum(cotangent.astype(jnp.float32), axis=(0, 1, 2))
    gain_total, shift_total, bias_total = lax.psum(
        (gain_product, shift_term, bias_term), ("fsdp", "dp")
    )
    return (
        output,
        feature_gradient,
        weight_grad,
        gain_total / images,
        shift_total / images,
        bias_total / images,
    )


def solution(mesh):
    in_specs = (
        P(("fsdp", "dp"), None, None, None),
        P("fsdp", None),
        P(),
        P(),
        P(),
        P(("fsdp", "dp"), None, None, None),
    )
    out_specs = (
        P(("fsdp", "dp"), None, None, None),
        P(("fsdp", "dp"), None, None, None),
        P("fsdp", None),
        P(),
        P(),
        P(),
    )
    return jax.shard_map(local, mesh=mesh, in_specs=in_specs, out_specs=out_specs, check_vma=False)
```

profile of v0, /device:TPU:64, one launch (start us, length us, event | category | flops | bytes accessed | tf_op | source)
XLA Modules:
  0.0 618.6 jit_solution(17690839852276540132)
XLA Ops:
  7.9 1.0 convert_reduce_fusion
  9.4 1.1 fusion.26
  10.8 103.8 %all-gather.3.cloned.1.call-done = bf16[32,20,5760]{2,1,0:T(8,128)(2,1)} async-done(((bf16[1,20,5760]{2,1,0:T(8,128)(2,1)}), bf16[32,20,5760]{2,1,0:T(8,128)(2,1)}) %all-gather.3.cloned.1.call-update) | async-done | bytes 7372816 | tf_op jit(solution)/shard_map/all_gather | solution.py:50
  114.6 9.2 %reshape.255 = bf16[640,5760]{1,0:T(8,128)(2,1)} reshape(bf16[32,20,5760]{2,1,0:T(8,128)(2,1)} %all-gather.3.cloned.1.call-done) | data formatting | bytes 14745600
  123.8 1.8 fusion.27
  125.6 2.0 convolution_add_fusion.7
  127.6 1.6 convolution_add_fusion.6
  129.3 1.6 convolution_add_fusion.5
  134.3 1.1 fusion.24
  135.4 1.6 bitcast_dynamic-update-slice_fusion.8
  137.0 1.6 bitcast_dynamic-update-slice_fusion.7
  138.6 1.7 bitcast_dynamic-update-slice_fusion.6
  140.3 1.6 bitcast_dynamic-update-slice_fusion.5
  141.9 1.7 bitcast_dynamic-update-slice_fusion.4
  143.6 1.6 bitcast_dynamic-update-slice_fusion.3
  145.2 1.7 bitcast_dynamic-update-slice_fusion.2
  146.9 1.6 bitcast_dynamic-update-slice_fusion.1
  148.6 1.6 bitcast_dynamic-update-slice_fusion
  152.2 1.6 fusion.28
  153.8 1.6 convolution_add_fusion.15
  155.4 1.6 convolution_add_fusion.14
  157.0 1.6 convolution_add_fusion.13
  158.6 1.8 convolution_add_fusion.12
  160.4 1.6 convolution_add_fusion.11
  162.0 1.6 convolution_add_fusion.10
  163.7 1.6 convolution_add_fusion.9
  165.3 341.2 %all-reduce.9.cloned.1.call-done = f32[640,5760]{0,1:T(8,128)} async-done(((f32[640,5760]{0,1:T(8,128)}), f32[640,5760]{0,1:T(8,128)}) %all-reduce.9.cloned.1.call-update) | async-done | bytes 14745616
  506.4 5.1 constant_dynamic-slice_fusion
  511.5 2.3 fusion.5
  513.9 92.7 %all-reduce.3 = (f32[640]{0:T(1024)S(1)}, f32[640]{0:T(1024)S(1)}, f32[640]{0:T(1024)S(1)}) all-reduce(f32[640]{0:T(1024)S(1)} %get-tuple-element.30, f32[640]{0:T(1024)S(1)} %get-tuple-element.33, f32[640]{0:T(1024)S(1)} %convert_reduce_fusion.1), channel_id=1, replica_groups=mesh['fsdp'=32,'dp'=8] {'fsdp','dp'}, use_global_device_ids=true, to_apply=%region_11.12 | all-reduce | flops 1920 | bytes 15360 | tf_op jit(solution)/shard_map/psum | solution.py:101
  607.8 2.0 broadcast_multiply_fusion
  609.8 2.3 copy.15
  (50 shorter events, 7.3 us)
Async XLA Ops:
  7.2 107.4 %all-gather.3.cloned.1.call-start = ((), (), s32[]{:S(2)}) async-start(), calls=%async_computation.1 | async-start | bytes 9123840 | tf_op jit(solution)/shard_map/all_gather | solution.py:50
  7.9 498.5 %all-reduce.9.cloned.1.call-start = ((), (), s32[]{:S(2)}) async-start(), calls=%async_computation.2 | async-start | bytes 29491200
  10.8 113.0 %copy-start = (bf16[1,16,16,640]{3,2,1,0:T(8,128)(2,1)S(1)}, bf16[1,16,16,640]{3,2,1,0:T(8,128)(2,1)}, u32[]{:S(2)}) copy-start(bf16[1,16,16,640]{3,2,1,0:T(8,128)(2,1)} %param.11) | copy-start | bytes 983044
  123.8 7.1 %copy-start.1 = (bf16[640,5760]{1,0:T(8,128)(2,1)S(1)}, bf16[640,5760]{1,0:T(8,128)(2,1)}, u32[]{:S(2)}) copy-start(bf16[640,5760]{1,0:T(8,128)(2,1)} %reshape.255) | copy-start | bytes 22118404
  127.6 5.2 copy-start.2
  127.6 5.2 copy-start.3
  127.6 5.2 copy-start.4
  150.2 0.7 copy-start.6
  150.2 457.6 %all-reduce.7.cloned.1.call-start = ((), (), s32[]{:S(2)}) async-start(), calls=%async_computation | async-start | bytes 5898240 | tf_op jit(solution)/shard_map/psum | solution.py:81
  162.0 349.5 %copy-start.5 = (f32[640]{0:T(1024)S(1)}, f32[640]{0:T(1024)}, u32[]{:S(2)}) copy-start(f32[640]{0:T(1024)} %param.10) | copy-start | bytes 7684
Sparse Core Ops, SparseCore 0:
  10.8 103.7 all-gather.2
  150.4 356.0 all-reduce.8
  511.7 94.9 all-reduce.6
where the time goes:
time: 620 us; the launch traced here: 619 us
  waiting for transfers between devices  446 us (72%)
  blocking collectives  92.7 us (15%)
  matrix products  39.8 us (6%)
  local copies, waits for them, and re-layouts  18.6 us (3%)
  between operations  14.7 us (2%)
  other arithmetic  6.97 us (1%)
    unnamed x4, waiting for transfers between devices  342 us
    all_gather x1, waiting for transfers between devices, local(): full_weight = lax.all_gather(weight, 'fsdp', axis=0, tiled=True)  104 us
    psum x1, blocking collectives, local(): lax.psum((gain_product, shift_term, bias_term), ('fsdp', 'dp'))  92.7 us
    unnamed x18, local copies, waits for them, and re-layouts  17.6 us
    dot_general x9, matrix products, local(): jnp.einsum('nijc,co->nijo', tap_window(hidden_pad, tap_index, side_len, F...  15.4 us
    dot_general x9, matrix products, local(): jnp.einsum('nijc,nijo->co', tap_window(hidden_pad, tap_index, side_len, F...  14.8 us
  transfers between devices with their start and end apart: 3, of which 2 were waited for; matrix products, arithmetic and copies ran while one was open for 3% of the time, Pallas kernels for 0%

commit v1 on v0

--- a/solution.py
+++ b/solution.py
@@ -77,8 +77,9 @@
             )
         )
     local_term = jnp.concatenate(columns, axis=1)
-    weight_sum = lax.psum_scatter(local_term, "fsdp", scatter_dimension=0, tiled=True)
-    weight_total = lax.psum(weight_sum, "dp")
+    local_term = local_term.reshape(lax.axis_size("fsdp"), -1, 9 * width_out)
+    weight_sum = lax.psum_scatter(local_term, "fsdp", scatter_dimension=0)
+    weight_total = lax.psum(weight_sum.astype(jnp.float32), "dp")
     weight_grad = weight_total / images
     sigmoid = jax.nn.sigmoid(preactivation)
     preactivation_gradient = grad_hidden * sigmoid * (1.0 + preactivation * (1.0 - sigmoid))

time: 620 us -> 483 us (0.78)
  waiting for transfers between devices: 446 us -> 307 us
  local copies, waits for them, and re-layouts: 18.6 us -> 38.6 us
  blocking collectives: 92.7 us -> 74.8 us
    unnamed x4, waiting for transfers between devices: 342 us -> 200 us
    psum x1, blocking collectives: 92.7 us -> 74.8 us  [local(): lax.psum((gain_product, shift_term, bias_term), ('fsdp', 'dp'))]
    concatenate x0 -> x1, local copies, waits for them, and re-layouts: none -> 15.2 us  [local(): local_term = jnp.concatenate(columns, axis=1)]
    reshape x0 -> x1, local copies, waits for them, and re-layouts: none -> 13.2 us  [local(): local_term = local_term.reshape(lax.axis_size('fsdp'), -1, 9 * width_out)]
    unnamed x18 -> x13, local copies, waits for them, and re-layouts: 17.6 us -> 9.22 us
  transfers between devices with their start and end apart: 3 -> 3, of which waited for: 2 -> 3; matrix products, arithmetic and copies ran while one was open for 3% -> 4% of each run, Pallas kernels for 0% -> 0%
where the time goes in v1:
time: 483 us; the launch traced here: 481 us
  waiting for transfers between devices  307 us (64%)
  blocking collectives  74.8 us (15%)
  matrix products  39.9 us (8%)
  local copies, waits for them, and re-layouts  38.6 us (8%)
  between operations  14 us (3%)
  other arithmetic  6.84 us (1%)
    unnamed x4, waiting for transfers between devices  200 us
    all_gather x1, waiting for transfers between devices, local(): full_weight = lax.all_gather(weight, 'fsdp', axis=0, tiled=True)  104 us
    psum x1, blocking collectives, local(): lax.psum((gain_product, shift_term, bias_term), ('fsdp', 'dp'))  74.8 us
    dot_general x9, matrix products, local(): jnp.einsum('nijc,co->nijo', tap_window(hidden_pad, tap_index, side_len, F...  15.5 us
    concatenate x1, local copies, waits for them, and re-layouts, local(): local_term = jnp.concatenate(columns, axis=1)  15.2 us
    dot_general x9, matrix products, local(): jnp.einsum('nijc,nijo->co', tap_window(hidden_pad, tap_index, side_len, F...  14.8 us
    reshape x1, local copies, waits for them, and re-layouts, local(): local_term = local_term.reshape(lax.axis_size('fsdp'), -1, 9 * width_out)  13.2 us
  transfers between devices with their start and end apart: 3, of which 3 were waited for; matrix products, arithmetic and copies ran while one was open for 4% of the time, Pallas kernels for 0%

profile of v1, /device:TPU:64, one launch (start us, length us, event | category | flops | bytes accessed | tf_op | source)
XLA Modules:
  0.0 481.2 jit_solution(8834222870870780972)
XLA Ops:
  9.4 1.1 fusion.26
  10.8 103.8 %all-gather.3.cloned.1.call-done = bf16[32,20,5760]{2,1,0:T(8,128)(2,1)} async-done(((bf16[1,20,5760]{2,1,0:T(8,128)(2,1)}), bf16[32,20,5760]{2,1,0:T(8,128)(2,1)}) %all-gather.3.cloned.1.call-update) | async-done | bytes 7372816 | tf_op jit(solution)/shard_map/all_gather | solution.py:50
  114.6 9.2 %reshape.259 = bf16[640,5760]{1,0:T(8,128)(2,1)} reshape(bf16[32,20,5760]{2,1,0:T(8,128)(2,1)} %all-gather.3.cloned.1.call-done) | data formatting | bytes 14745600
  123.8 1.8 fusion.27
  125.6 2.0 convolution_add_fusion.7
  127.6 1.7 convolution_add_fusion.6
  129.3 1.6 convolution_add_fusion.5
  134.3 1.1 fusion.24
  135.4 1.6 bitcast_dynamic-update-slice_fusion.8
  137.0 1.6 bitcast_dynamic-update-slice_fusion.7
  138.6 1.6 bitcast_dynamic-update-slice_fusion.6
  140.3 1.7 bitcast_dynamic-update-slice_fusion.5
  141.9 1.6 bitcast_dynamic-update-slice_fusion.4
  143.6 1.7 bitcast_dynamic-update-slice_fusion.3
  145.3 1.6 bitcast_dynamic-update-slice_fusion.2
  146.9 1.7 bitcast_dynamic-update-slice_fusion.1
  148.6 1.6 bitcast_dynamic-update-slice_fusion
  150.2 15.2 %copy.15 = f32[640,5760]{1,0:T(8,128)} copy(f32[640,5760]{0,1:T(8,128)} %bitcast_dynamic-update-slice_fusion) | data formatting | bytes 29491200 | tf_op jit(solution)/shard_map/concatenate | solution.py:79
  165.4 13.2 %reshape.257 = f32[32,20,5760]{2,1,0:T(8,128)} reshape(f32[640,5760]{1,0:T(8,128)} %copy.15) | data formatting | bytes 29491200 | tf_op jit(solution)/shard_map/reshape | solution.py:80
  178.9 1.6 fusion.28
  180.5 1.6 convolution_add_fusion.15
  182.1 1.6 convolution_add_fusion.14
  183.8 1.6 convolution_add_fusion.13
  185.4 1.6 convolution_add_fusion.12
  187.0 1.6 convolution_add_fusion.11
  188.6 1.8 convolution_add_fusion.10
  190.4 1.7 convolution_add_fusion.9
  192.1 198.8 %reduce-scatter.4.cloned.1.call-done = f32[1,20,5760]{2,1,0:T(8,128)} async-done(((f32[32,20,5760]{2,1,0:T(8,128)}), f32[1,20,5760]{2,1,0:T(8,128)}) %reduce-scatter.4.cloned.1.call-update) | async-done | bytes 460816
  391.0 2.3 fusion.5
  393.3 74.8 %all-reduce.3 = (f32[640]{0:T(1024)S(1)}, f32[640]{0:T(1024)S(1)}, f32[640]{0:T(1024)S(1)}) all-reduce(f32[640]{0:T(1024)S(1)} %get-tuple-element.6, f32[640]{0:T(1024)S(1)} %get-tuple-element.9, f32[640]{0:T(1024)S(1)} %convert_reduce_fusion.1), channel_id=1, replica_groups=mesh['fsdp'=32,'dp'=8] {'fsdp','dp'}, use_global_device_ids=true, to_apply=%region_11.12 | all-reduce | flops 1920 | bytes 15360 | tf_op jit(solution)/shard_map/psum | solution.py:102
  469.3 3.5 all-reduce.6.cloned.1.call-done
  472.8 1.9 broadcast_multiply_fusion
  (47 shorter events, 7.4 us)
Async XLA Ops:
  7.2 107.4 %all-gather.3.cloned.1.call-start = ((), (), s32[]{:S(2)}) async-start(), calls=%async_computation.2 | async-start | bytes 9123840 | tf_op jit(solution)/shard_map/all_gather | solution.py:50
  7.9 383.0 %reduce-scatter.4.cloned.1.call-start = ((), (), s32[]{:S(2)}) async-start(), calls=%async_computation.3 | async-start | bytes 18247680
  10.8 113.0 %copy-start = (bf16[1,16,16,640]{3,2,1,0:T(8,128)(2,1)S(1)}, bf16[1,16,16,640]{3,2,1,0:T(8,128)(2,1)}, u32[]{:S(2)}) copy-start(bf16[1,16,16,640]{3,2,1,0:T(8,128)(2,1)} %param.11) | copy-start | bytes 983044
  123.8 7.1 %copy-start.1 = (bf16[640,5760]{1,0:T(8,128)(2,1)S(1)}, bf16[640,5760]{1,0:T(8,128)(2,1)}, u32[]{:S(2)}) copy-start(bf16[640,5760]{1,0:T(8,128)(2,1)} %reshape.259) | copy-start | bytes 22118404
  127.6 5.2 %copy-start.2 = (bf16[1,16,16,640]{3,2,1,0:T(8,128)(2,1)S(1)}, bf16[1,16,16,640]{3,2,1,0:T(8,128)(2,1)}, u32[]{:S(2)}) copy-start(bf16[1,16,16,640]{3,2,1,0:T(8,128)(2,1)} %param.6) | copy-start | bytes 983044
  127.6 5.2 %copy-start.3 = (f32[640]{0:T(1024)S(1)}, f32[640]{0:T(1024)}, u32[]{:S(2)}) copy-start(f32[640]{0:T(1024)} %param.8) | copy-start | bytes 7684
  127.6 5.2 %copy-start.4 = (f32[640]{0:T(1024)S(1)}, f32[640]{0:T(1024)}, u32[]{:S(2)}) copy-start(f32[640]{0:T(1024)} %param.9) | copy-start | bytes 7684
  178.6 294.2 %all-reduce.6.cloned.1.call-start = ((), (), s32[]{:S(2)}) async-start(), calls=%async_computation.1 | async-start | bytes 1105920 | tf_op jit(solution)/shard_map/psum | solution.py:82
  182.1 208.8 %copy-start.5 = (f32[640]{0:T(1024)S(1)}, f32[640]{0:T(1024)}, u32[]{:S(2)}) copy-start(f32[640]{0:T(1024)} %param.10) | copy-start | bytes 7684
Sparse Core Ops, SparseCore 0:
  10.8 103.7 all-gather.2
  178.7 212.1 reduce-scatter.3
  393.6 79.1 all-reduce.5

commit v2 on v0

v2 whole, which is shorter than its diff:
```python
import functools

import jax
import jax.numpy as jnp
import numpy as np
from jax import lax
from jax.experimental import pallas as pl
from jax.experimental.pallas import tpu as pltpu
from jax.sharding import PartitionSpec as P

MESH = pl.DeviceIdType.MESH
F32 = jnp.float32
BF16 = jnp.bfloat16
EPS = 1e-05
C = 640
GROUP = 40
SIDE = 16
PIX = SIDE * SIDE
CH = 384
NZ = 8
BLK = 320
ENTRIES = float(PIX * GROUP)
IMAGES = 256.0

ZW, AGB, AGA, RSA, RSB, SIB, SW, PC, FIN, V1, V2, V3, NSEM = (
    0, 16, 22, 28, 34, 40, 42, 50, 58, 74, 90, 94, 98)


def kernel(feat, w, par, cot, perm, ind, indt, out, fg, wg, vec,
           zbuf, mf, wall, term, xs, ds, hb, ht, cc, cb, pbuf, gh,
           o1, r1, ub, o2, r2, vb, cr, f2, rf, vs, v1, v2, v3, ss, rs):
    fi = lax.axis_index("fsdp")
    di = lax.axis_index("dp")
    z = fi // 4
    h = (fi // 2) % 2
    s = fi % 2
    lo = di // 4
    x = di % 4
    y = h * 2 + lo
    ra = (1 - s) * x + s * y
    rb = (1 - s) * y + s * x

    def dev(xx, yy, zz, sc):
        return {"fsdp": (zz * 2 + yy // 2) * 2 + sc, "dp": (yy % 2) * 4 + xx}

    def rc(src, dst, i, device):
        return pltpu.make_async_remote_copy(
            src_ref=src, dst_ref=dst, send_sem=ss.at[i], recv_sem=rs.at[i],
            device_id=device, device_id_type=MESH)

    sib = dev(x, y, z, 1 - s)
    a_right = dev((x + 1 - s) % 4, (y + s) % 4, z, s)
    a_left = dev((x + 3 * (1 - s)) % 4, (y + 3 * s) % 4, z, s)
    b_right = dev((x + s) % 4, (y + 1 - s) % 4, z, s)
    b_left = dev((x + 3 * s) % 4, (y + 3 * (1 - s)) % 4, z, s)
    zpeers = [(dz, dc) for dz in range(NZ) for dc in range(2) if (dz, dc) != (0, 0)]
    fpeers = [(dl, dx, dc) for dl in range(2) for dx in range(4) for dc in range(2)
              if (dl, dx, dc) != (0, 0, 0)]

    def zdev(dz, dc):
        return dev(x, y, (z + dz) % NZ, (s + dc) % 2)

    def fdev(dl, dx, dc):
        return dev((x + dx) % 4, h * 2 + (lo + dl) % 2, z, (s + dc) % 2)

    barrier = pltpu.get_barrier_semaphore()
    everyone = [zdev(*p) for p in zpeers] + [fdev(*p) for p in fpeers]
    everyone += [dev(x, (y + k) % 4, z, s) for k in (1, 2, 3)]
    for device in everyone:
        pl.semaphore_signal(barrier, inc=1, device_id=device, device_id_type=MESH)
    pl.semaphore_wait(barrier, len(everyone))

    def wcols(sc):
        k = jnp.minimum(sc * 8 + lo * 4 + x, 14)
        return w.at[:, pl.ds(pl.multiple_of(k * CH, CH), CH)]

    zc = []
    for dz, dc in zpeers:
        cp = rc(wcols((s + dc) % 2), zbuf.at[z * 2 + s], ZW + dz * 2 + dc, zdev(dz, dc))
        cp.start()
        zc.append(cp)
    own = pltpu.make_async_copy(wcols(s), zbuf.at[z * 2 + s], ss.at[ZW])
    own.start()

    pj = lax.broadcasted_iota(jnp.int32, (PIX, C), 0) % SIDE
    first, last = pj == 0, pj == SIDE - 1
    ct = cot[...].astype(F32)
    vs[2] = jnp.sum(ct, axis=0, keepdims=True) * jnp.ones((8, 1), F32)
    zero16 = jnp.zeros((SIDE, C), BF16)
    for b in range(3):
        cb[b, 0:SIDE, :] = zero16
        cb[b, SIDE + PIX:, :] = zero16
    cb[1, SIDE:SIDE + PIX, :] = cot[...]
    cb[2, SIDE:SIDE + PIX, :] = jnp.where(first, 0.0, pltpu.roll(ct, 1, 0)).astype(BF16)
    cb[0, SIDE:SIDE + PIX, :] = jnp.where(last, 0.0, pltpu.roll(ct, PIX - 1, 0)).astype(BF16)
    for tile in range(45):
        t, ot = divmod(tile, 5)
        a, b = divmod(t, 3)
        k, i = divmod(tile, 3)
        cc[k, 0:PIX, i * 128:(i + 1) * 128] = cb[
            b, SIDE * (2 - a):SIDE * (2 - a) + PIX, ot * 128:(ot + 1) * 128]
    cc[15, 0:PIX, :] = jnp.zeros((PIX, CH), BF16)
    theirs = pl.ds((1 - s) * 8, 8)
    sib_c = rc(cc.at[theirs, pl.ds(0, PIX)], cc.at[theirs, pl.ds(PIX, PIX)], SIB, sib)
    sib_c.start()

    def grouped(row):
        rows = jnp.broadcast_to(row, (8, C))
        small = jnp.dot(rows, ind[...], precision=lax.Precision.HIGHEST, preferred_element_type=F32)
        return jnp.dot(small, indt[...], precision=lax.Precision.HIGHEST,
                       preferred_element_type=F32)[0:1] / ENTRIES

    gain, shift, bias = par[0:1, :], par[1:2, :], par[2:3, :]
    xs[...] = jnp.dot(feat[...], perm[...], preferred_element_type=F32)
    mu = grouped(jnp.sum(xs[...], axis=0, keepdims=True))
    centred = xs[...] - mu
    xs[...] = centred
    inverse = lax.rsqrt(grouped(jnp.sum(centred * centred, axis=0, keepdims=True)) + EPS)
    xhat = xs[...] * inverse
    xs[...] = xhat
    pre = xhat * gain + shift
    sg = 1.0 / (1.0 + jnp.exp(-pre))
    ds[...] = sg * (1.0 + pre * (1.0 - sg))
    hid = pre * sg
    hb[...] = hid.astype(BF16)
    ht[:, 0:PIX] = hid.T.astype(BF16)
    sib_h = rc(ht.at[:, pl.ds(0, PIX)], ht.at[:, pl.ds(PIX, PIX)], SIB + 1, sib)
    sib_h.start()

    own.wait()
    for cp in zc:
        cp.wait_recv()
    for q in range(16):
        mf[q * 20:(q + 1) * 20, :] = zbuf[q].astype(F32)
    me = s * 16 + ra * 4 + rb
    wall[me] = mf[...].astype(BF16)

    def ring_gather(pos, right, left, piece, base):
        rt, lf = (pos + 1) % 4, (pos + 3) % 4
        first_sends = [
            rc(piece(pos, 0), piece(pos, 0), base, right),
            rc(piece(pos, 1), piece(pos, 1), base + 1, left),
            rc(piece(pos, 1), piece(pos, 1), base + 2, right),
            rc(piece(pos, 0), piece(pos, 0), base + 3, left),
        ]
        for cp in first_sends:
            cp.start()

        def relay(arrived):
            first_sends[0].wait_recv()
            f0 = rc(piece(lf, 0), piece(lf, 0), base + 4, right)
            f0.start()
            first_sends[1].wait_recv()
            f1 = rc(piece(rt, 1), piece(rt, 1), base + 5, left)
            f1.start()
            arrived(lf, 0, 1)
            arrived(rt, 1, 2)

            def finish():
                first_sends[2].wait_recv()
                arrived(lf, 1, 1)
                first_sends[3].wait_recv()
                arrived(rt, 0, 2)
                opp = (pos + 2) % 4
                f0.wait_recv()
                arrived(opp, 0, 3)
                f1.wait_recv()
                arrived(opp, 1, 3)
                for cp in first_sends + [f0, f1]:
                    cp.wait_send()
            return finish
        return relay

    def piece_b(j, half):
        return wall.at[s * 16 + ra * 4 + j, pl.ds(half * 160, 160)]

    def piece_a(j, half):
        return wall.at[pl.ds(s * 16 + j * 4 + half * 2, 2)]

    relay_b = ring_gather(rb, b_right, b_left, piece_b, AGB)

    sib_c.wait_recv()
    sib_h.wait_recv()

    def wgrad(i):
        res = jnp.dot(ht[...], cc[s * 8 + i], preferred_element_type=F32).astype(BF16)
        l2, xx = i // 4, i % 4
        for hh in range(2):
            yy = hh * 2 + l2
            idx = (1 - s) * (xx * 4 + yy) + s * (yy * 4 + xx)
            term[idx] = res[hh * BLK:(hh + 1) * BLK]

    pl.loop(0, 3)(wgrad)
    finish_b = relay_b(lambda j, half, rel: None)
    pl.loop(3, 5)(wgrad)
    finish_b()

    sib_w = []

    def to_sibling(j, half, rel):
        cp = rc(piece_a(j, half), piece_a(j, half), SW + rel * 2 + half, sib)
        cp.start()
        sib_w.append(cp)

    relay_a = ring_gather(ra, a_right, a_left, piece_a, AGA)
    to_sibling(ra, 0, 0)
    to_sibling(ra, 1, 0)
    pl.loop(5, 8)(wgrad)

    def ring_reduce(pos, right, left, piece, o, r, base, add):
        rt, lf, opp = (pos + 1) % 4, (pos + 3) % 4, (pos + 2) % 4
        sends = [
            rc(piece(opp, 0), o(0), base, right),
            rc(piece(opp, 1), o(1), base + 1, left),
            rc(piece(rt, 1), r(0, 1), base + 2, right),
            rc(piece(lf, 0), r(1, 0), base + 3, left),
        ]
        for cp in sends:
            cp.start()

        def middle():
            sends[0].wait_recv()
            add(rt, 0)
            g0 = rc(piece(rt, 0), r(0, 0), base + 4, right)
            g0.start()
            sends[1].wait_recv()
            add(lf, 1)
            g1 = rc(piece(lf, 1), r(1, 1), base + 5, left)
            g1.start()

            def finish():
                for cp in (sends[2], sends[3], g0, g1):
                    cp.wait_recv()
                for cp in sends + [g0, g1]:
                    cp.wait_send()
            return finish
        return middle

    def add_a(j, half):
        @pl.loop(0, 2)
        def _(q):
            at = j * 4 + half * 2 + q
            term[at] = (term[at].astype(F32) + o1[half * 2 + q].astype(F32)).astype(BF16)

    middle_ra = ring_reduce(
        ra, a_right, a_left,
        lambda j, half: term.at[pl.ds(j * 4 + half * 2, 2)],
        lambda half: o1.at[pl.ds(half * 2, 2)],
        lambda side, half: r1.at[side, pl.ds(half * 2, 2)],
        RSA, add_a)

    finish_a = relay_a(to_sibling)
    finish_a()
    finish_ra = middle_ra()

    gh[...] = jnp.zeros((PIX, C), F32)

    def conv(sc, i):
        l2, xx = i // 4, i % 4
        rows = []
        for hh in range(2):
            yy = hh * 2 + l2
            rows.append(wall[sc * 16 + (1 - sc) * (xx * 4 + yy) + sc * (yy * 4 + xx)])
        wk = jnp.concatenate(rows, axis=0)
        k = sc * 8 + i
        pbuf[k] = jnp.dot(hb[...], wk, preferred_element_type=F32)
        gh[...] += lax.dot_general(cc[k, 0:PIX], wk, (((1,), (1,)), ((), ())),
                                   preferred_element_type=F32)

    pl.loop(0, 8)(functools.partial(conv, s))
    for cp in sib_w:
        cp.wait_recv()
    pl.loop(0, 8)(functools.partial(conv, 1 - s))

    gp = gh[...] * ds[...]
    gh[...] = gp
    shift_sum = jnp.sum(gp, axis=0, keepdims=True)
    gain_sum = jnp.sum(gp * xs[...], axis=0, keepdims=True)
    vs[0] = jnp.broadcast_to(gain_sum, (8, C))
    vs[1] = jnp.broadcast_to(shift_sum, (8, C))
    row = lax.broadcasted_iota(jnp.int32, (8, C), 0)
    vs[3] = jnp.where(row == 0, vs[0], jnp.where(row == 1, vs[1], vs[2]))
    v1[z * 2 + s] = vs[3]
    vc = []
    for dz, dc in zpeers:
        cp = rc(vs.at[3], v1.at[z * 2 + s], V1 + dz * 2 + dc, zdev(dz, dc))
        cp.start()
        vc.append(cp)
    m1 = grouped(shift_sum * gain)
    m2 = grouped(gain_sum * gain)
    g = gh[...] * gain
    fgp = ((g - m1 - xs[...] * m2) * inverse).astype(BF16)
    fg[...] = lax.dot_general(fgp, perm[...], (((1,), (1,)), ((), ())),
                              preferred_element_type=F32).astype(BF16)

    finish_ra()
    for j in range(4):
        ub[j] = (term[ra * 4 + j].astype(F32) + r1[0, j].astype(F32)
                 + r1[1, j].astype(F32)).astype(BF16)

    def add_b(j, half):
        part = pl.ds(half * 160, 160)
        ub[j, part] = (ub[j, part].astype(F32) + o2[half].astype(F32)).astype(BF16)

    middle_rb = ring_reduce(
        rb, b_right, b_left,
        lambda j, half: ub.at[j, pl.ds(half * 160, 160)],
        lambda half: o2.at[half],
        lambda side, half: r2.at[side, pl.ds(half * 160, 160)],
        RSB, add_b)

    for cp in vc:
        cp.wait_recv()
    vs[4] = jnp.sum(v1[...], axis=0)
    v2[x] = vs[4]
    vx = []
    for k in (1, 2, 3):
        cp = rc(vs.at[4], v2.at[x], V2 + k, dev((x + k) % 4, y, z, s))
        cp.start()
        vx.append(cp)
    finish_rb = middle_rb()

    for ot in range(5):
        total = None
        for b in range(3):
            parts = []
            for a in range(3):
                k, i = divmod(5 * (3 * a + b) + ot, 3)
                p = pbuf[k, :, i * 128:(i + 1) * 128]
                pad = jnp.zeros((SIDE, 128), F32)
                if a == 0:
                    p = jnp.concatenate([pad, p[:PIX - SIDE]], axis=0)
                elif a == 2:
                    p = jnp.concatenate([p[SIDE:], pad], axis=0)
                parts.append(p)
            sb = parts[0] + parts[1] + parts[2]
            if b == 0:
                sb = jnp.where(first[:, :128], 0.0, pltpu.roll(sb, 1, 0))
            elif b == 2:
                sb = jnp.where(last[:, :128], 0.0, pltpu.roll(sb, PIX - 1, 0))
            total = sb if total is None else total + sb
        cols = slice(ot * 128, (ot + 1) * 128)
        out[:, cols] = (total + bias[:, cols]).astype(BF16)

    for cp in vx:
        cp.wait_recv()
    vs[5] = jnp.sum(v2[...], axis=0)
    v3[y] = vs[5]
    vy = []
    for k in (1, 2, 3):
        cp = rc(vs.at[5], v3.at[y], V3 + k, dev(x, (y + k) % 4, z, s))
        cp.start()
        vy.append(cp)

    finish_rb()
    total = ub[rb].astype(F32) + r2[0].astype(F32) + r2[1].astype(F32)
    for q in range(NZ):
        vb[q] = total[q * 40:(q + 1) * 40].astype(BF16)
    cr[z] = vb[z]
    pc = []
    for dz in range(1, NZ):
        cp = rc(vb.at[(z + dz) % NZ], cr.at[z], PC + dz, dev(x, y, (z + dz) % NZ, s))
        cp.start()
        pc.append(cp)
    for cp in vy:
        cp.wait_recv()
    vec[...] = jnp.sum(v3[...], axis=0) / IMAGES
    for cp in pc:
        cp.wait_recv()
    full = jnp.sum(cr[...].astype(F32), axis=0) / IMAGES
    f2[0] = full[0:20]
    f2[1] = full[20:40]
    slot = s * 8 + lo * 4 + x
    rf[slot] = f2[s]
    fc = []
    for dl, dx, dc in fpeers:
        cp = rc(f2.at[(s + dc) % 2], rf.at[slot], FIN + dl * 8 + dx * 2 + dc, fdev(dl, dx, dc))
        cp.start()
        fc.append(cp)
    for cp in fc:
        cp.wait_recv()
    for k in range(15):
        wg[:, k * CH:(k + 1) * CH] = rf[k]
    for cp in zc + [sib_c, sib_h] + sib_w + vc + vx + vy + pc + fc:
        cp.wait_send()


def local(features, weight, gain, shift, bias, cotangent):
    def to_inner(v):
        return v.reshape(NZ, 2, GROUP).transpose(1, 0, 2).reshape(C)

    def to_outer(v):
        return v.reshape(2, NZ, GROUP).transpose(1, 0, 2).reshape(C)

    par = jnp.stack([to_inner(gain), to_inner(shift), bias] + [bias] * 5)
    order = np.arange(C).reshape(NZ, 2, GROUP).transpose(1, 0, 2).reshape(C)
    perm = np.zeros((C, C), np.float32)
    perm[order, np.arange(C)] = 1.0
    ind = np.zeros((C, 128), np.float32)
    ind[np.arange(C), np.arange(C) // GROUP] = 1.0
    vm = pl.BlockSpec(memory_space=pltpu.VMEM)
    out, fg, wg, vec = pl.pallas_call(
        kernel,
        name="fused_step",
        out_shape=[
            jax.ShapeDtypeStruct((PIX, C), BF16),
            jax.ShapeDtypeStruct((PIX, C), BF16),
            jax.ShapeDtypeStruct((20, 9 * C), F32),
            jax.ShapeDtypeStruct((8, C), F32),
        ],
        in_specs=[vm] * 7,
        out_specs=[vm] * 4,
        scratch_shapes=[
            pltpu.VMEM((16, 20, CH), BF16),
            pltpu.VMEM((BLK, CH), F32),
            pltpu.VMEM((32, BLK, CH), BF16),
            pltpu.VMEM((16, BLK, CH), BF16),
            pltpu.VMEM((PIX, C), F32),
            pltpu.VMEM((PIX, C), F32),
            pltpu.VMEM((PIX, C), BF16),
            pltpu.VMEM((C, 2 * PIX), BF16),
            pltpu.VMEM((16, 2 * PIX, CH), BF16),
            pltpu.VMEM((3, PIX + 2 * SIDE, C), BF16),
            pltpu.VMEM((16, PIX, CH), F32),
            pltpu.VMEM((PIX, C), F32),
            pltpu.VMEM((4, BLK, CH), BF16),
            pltpu.VMEM((2, 4, BLK, CH), BF16),
            pltpu.VMEM((4, BLK, CH), BF16),
            pltpu.VMEM((2, 160, CH), BF16),
            pltpu.VMEM((2, BLK, CH), BF16),
            pltpu.VMEM((NZ, 40, CH), BF16),
            pltpu.VMEM((NZ, 40, CH), BF16),
            pltpu.VMEM((2, 20, CH), F32),
            pltpu.VMEM((16, 20, CH), F32),
            pltpu.VMEM((6, 8, C), F32),
            pltpu.VMEM((16, 8, C), F32),
            pltpu.VMEM((4, 8, C), F32),
            pltpu.VMEM((4, 8, C), F32),
            pltpu.SemaphoreType.DMA((NSEM,)),
            pltpu.SemaphoreType.DMA((NSEM,)),
        ],
        compiler_params=pltpu.CompilerParams(
            collective_id=0, has_side_effects=True, vmem_limit_bytes=60 * 1024 * 1024),
    )(features.reshape(PIX, C), weight, par, cotangent.reshape(PIX, C),
      jnp.asarray(perm, BF16), jnp.asarray(ind), jnp.asarray(ind.T.copy()))
    shape = features.shape
    return (out.reshape(shape), fg.reshape(shape), wg,
            to_outer(vec[0]), to_outer(vec[1]), vec[2])


def solution(mesh):
    img = P(("fsdp", "dp"), None, None, None)
    return jax.shard_map(
        local, mesh=mesh,
        in_specs=(img, P("fsdp", None), P(), P(), P(), img),
        out_specs=(img, img, P("fsdp", None), P(), P(), P()),
        check_vma=False)
```

time: 620 us -> 111 us (0.18)
  waiting for transfers between devices: 446 us -> 0 us
  Pallas kernels: 0 us -> 100 us
  blocking collectives: 92.7 us -> 0 us
  matrix products: 39.8 us -> 0 us
  between operations: 14.7 us -> 0.72 us
  local copies, waits for them, and re-layouts: 18.6 us -> 8.6 us
  other arithmetic: 6.97 us -> 0 us
    unnamed x4 -> x0, waiting for transfers between devices: 342 us -> none
    all_gather x1 -> x0, waiting for transfers between devices: 104 us -> none  [local(): full_weight = lax.all_gather(weight, 'fsdp', axis=0, tiled=True)]
    pallas_call x0 -> x1, Pallas kernels: none -> 100 us  [local(): pl.pallas_call(kernel, name='fused_step', out_shape=[jax.ShapeDtypeStruct...]
    psum x1 -> x0, blocking collectives: 92.7 us -> none  [local(): lax.psum((gain_product, shift_term, bias_term), ('fsdp', 'dp'))]
    dot_general x27 -> x0, matrix products: 39.8 us -> none  [the longest x9 15.4 us: local(): jnp.einsum('nijc,co->nijo', tap_window(hidden_pad, tap_index, side_len, F...]
    unnamed x18 -> x11, local copies, waits for them, and re-layouts: 17.6 us -> 3.92 us
  transfers between devices with their start and end apart: 3 -> 0, of which waited for: 2 -> 0; matrix products, arithmetic and copies ran while one was open for 3% -> 0% of each run, Pallas kernels for 0% -> 0%
where the time goes in v2:
time: 111 us; the launch traced here: 109 us
  Pallas kernels  100 us (90%)
  local copies, waits for them, and re-layouts  8.6 us (8%)
    pallas_call x1, Pallas kernels, local(): pl.pallas_call(kernel, name='fused_step', out_shape=[jax.ShapeDtypeStruct...  100 us
    unnamed x11, local copies, waits for them, and re-layouts  3.92 us

profile of v2, /device:TPU:64, one launch (start us, length us, event | category | flops | bytes accessed | tf_op | source)
XLA Modules:
  0.0 109.4 jit_solution(4927782486947423525)
XLA Ops:
  0.6 0.0 copy-start.2
  0.6 0.7 stack.4
  1.3 0.0 copy-done.2
  1.3 0.1 reshape.37
  1.4 0.0 copy-start.3
  1.5 0.1 stack_reshape.6
  1.5 0.6 copy-done.3
  2.1 0.1 reshape.38
  2.2 0.1 stack_reshape.7
  2.3 0.6 stack.5.par
  3.0 100.1 %fused_step.1 = (bf16[256,640]{1,0:T(8,128)(2,1)}, bf16[256,640]{1,0:T(8,128)(2,1)}, f32[20,5760]{1,0:T(8,128)}, f32[8,640]{1,0:T(8,128)}) custom-call(bf16[256,640]{1,0:T(8,128)(2,1)} %bitcast.14, bf16[20,5760]{1,0:T(8,128)(2,1)} %w.1, f32[8,640]{1,0:T(8,128)} %stack.5.par, bf16[256,640]{1,0:T(8,128)(2,1)} %bitcast.15, ...), custom_call_target="tpu_custom_call" | custom-call | tf_op jit(solution)/shard_map/fused_step/pallas_call | solution.py:402
  103.1 1.5 %slice_reduce_fusion = (f32[640]{0:T(1024)}, f32[640]{0:T(1024)S(1)}, f32[640]{0:T(1024)S(1)}) fusion(f32[8,640]{1,0:T(8,128)} %get-tuple-element.13), kind=kLoop, calls=%fused_computation.2 | loop fusion | bytes 15360 | tf_op jit(solution)/shard_map/slice | solution.py:448
  104.5 0.1 reshape_squeeze.7
  104.6 0.7 reshape.43
  105.3 0.1 reshape_squeeze.6
  105.4 0.0 copy-start.1
  105.4 0.7 reshape.42
  106.1 0.0 copy-start
  106.1 1.8 %copy.26 = bf16[1,16,16,640]{3,2,1,0:T(8,128)(2,1)} copy(bf16[1,16,16,640]{3,2,1,0:T(8,128)(2,1)} %bitcast.13) | data formatting | bytes 655360
  107.9 0.0 copy-done.1
  107.9 0.7 copy.27
  108.6 0.0 copy-done
  108.6 0.8 copy.28
  (4 shorter events, 0.0 us)
Async XLA Ops:
  0.6 0.7 copy-start.2
  1.4 0.7 copy-start.3
  105.4 2.5 %copy-start.1 = (bf16[256,640]{1,0:T(8,128)(2,1)S(1)}, bf16[256,640]{1,0:T(8,128)(2,1)}, u32[]{:S(2)}) copy-start(bf16[256,640]{1,0:T(8,128)(2,1)} %get-tuple-element.11) | copy-start | bytes 983044
  106.1 2.5 %copy-start = (f32[20,5760]{1,0:T(8,128)S(1)}, f32[20,5760]{1,0:T(8,128)}, u32[]{:S(2)}) copy-start(f32[20,5760]{1,0:T(8,128)} %get-tuple-element.25) | copy-start | bytes 1382404

commit v3 on v2

v3 whole, which is shorter than its diff:
```python
import functools

import jax
import jax.numpy as jnp
import numpy as np
from jax import lax
from jax.experimental import pallas as pl
from jax.experimental.pallas import tpu as pltpu
from jax.sharding import PartitionSpec as P

MESH = pl.DeviceIdType.MESH
F32 = jnp.float32
BF16 = jnp.bfloat16
EPS = 1e-05
C = 640
GROUP = 40
SIDE = 16
PIX = SIDE * SIDE
CH = 384
NZ = 8
BLK = 320
ENTRIES = float(PIX * GROUP)
IMAGES = 256.0

ZW, AGB, AGA, RSA, RSB, SIB, SW, PC, FIN, V1, V2, V3, NSEM = (
    0, 16, 22, 28, 34, 40, 42, 50, 58, 74, 90, 94, 98)


def kernel(feat, w, p_gain, p_shift, p_bias, cot, perm, ind, indt,
           out, fg, wg, out_gain, out_shift, out_bias,
           zbuf, mf, wall, term, xs, ds, hb, ht, cc, cb, pbuf, gh,
           o1, r1, ub, o2, r2, vb, cr, tf, f2, rf, vs, v1, v2, v3, scot, vo, ss, rs):
    fi = lax.axis_index("fsdp")
    di = lax.axis_index("dp")
    z = fi // 4
    h = (fi // 2) % 2
    s = fi % 2
    lo = di // 4
    x = di % 4
    y = h * 2 + lo
    ra = (1 - s) * x + s * y
    rb = (1 - s) * y + s * x

    def dev(xx, yy, zz, sc):
        return {"fsdp": (zz * 2 + yy // 2) * 2 + sc, "dp": (yy % 2) * 4 + xx}

    def rc(src, dst, i, device):
        return pltpu.make_async_remote_copy(
            src_ref=src, dst_ref=dst, send_sem=ss.at[i], recv_sem=rs.at[i],
            device_id=device, device_id_type=MESH)

    sib = dev(x, y, z, 1 - s)
    a_right = dev((x + 1 - s) % 4, (y + s) % 4, z, s)
    a_left = dev((x + 3 * (1 - s)) % 4, (y + 3 * s) % 4, z, s)
    b_right = dev((x + s) % 4, (y + 1 - s) % 4, z, s)
    b_left = dev((x + 3 * s) % 4, (y + 3 * (1 - s)) % 4, z, s)
    zpeers = [(dz, dc) for dz in range(NZ) for dc in range(2) if (dz, dc) != (0, 0)]
    fpeers = [(dl, dx, dc) for dl in range(2) for dx in range(4) for dc in range(2)
              if (dl, dx, dc) != (0, 0, 0)]

    def zdev(dz, dc):
        return dev(x, y, (z + dz) % NZ, (s + dc) % 2)

    def fdev(dl, dx, dc):
        return dev((x + dx) % 4, h * 2 + (lo + dl) % 2, z, (s + dc) % 2)

    barrier = pltpu.get_barrier_semaphore()
    everyone = [zdev(*p) for p in zpeers] + [fdev(*p) for p in fpeers]
    everyone += [dev(x, (y + k) % 4, z, s) for k in (1, 2, 3)]
    for device in everyone:
        pl.semaphore_signal(barrier, inc=1, device_id=device, device_id_type=MESH)

    pj = lax.broadcasted_iota(jnp.int32, (PIX, C), 0) % SIDE
    first, last = pj == 0, pj == SIDE - 1
    zero16 = jnp.zeros((SIDE, C), BF16)
    for b in range(3):
        cb[b, 0:SIDE, :] = zero16
        cb[b, SIDE + PIX:, :] = zero16

    def windows(source, at):
        wide = source[...].astype(F32)
        cb[1, SIDE:SIDE + PIX, :] = source[...]
        cb[2, SIDE:SIDE + PIX, :] = jnp.where(first, 0.0, pltpu.roll(wide, 1, 0)).astype(BF16)
        cb[0, SIDE:SIDE + PIX, :] = jnp.where(last, 0.0, pltpu.roll(wide, PIX - 1, 0)).astype(BF16)
        for tile in range(45):
            t, ot = divmod(tile, 5)
            a, b = divmod(t, 3)
            k, i = divmod(tile, 3)
            cc[k, at:at + PIX, i * 128:(i + 1) * 128] = cb[
                b, SIDE * (2 - a):SIDE * (2 - a) + PIX, ot * 128:(ot + 1) * 128]
        cc[15, at:at + PIX, :] = jnp.zeros((PIX, CH), BF16)
        return jnp.sum(wide, axis=0, keepdims=True)

    bias_sum = windows(cot, 0)
    for i in range(5):
        vs[0, 10 + i:11 + i, :] = bias_sum[:, i * 128:(i + 1) * 128]
    vs[0, 15:16, :] = jnp.zeros((1, 128), F32)
    pl.semaphore_wait(barrier, len(everyone))
    sib_c = rc(cot, scot, SIB, sib)
    sib_c.start()
    def wcols(sc):
        k = jnp.minimum(sc * 8 + lo * 4 + x, 14)
        return w.at[:, pl.ds(pl.multiple_of(k * CH, CH), CH)]

    zc = []
    for dz, dc in zpeers:
        cp = rc(wcols((s + dc) % 2), zbuf.at[z * 2 + s], ZW + dz * 2 + dc, zdev(dz, dc))
        cp.start()
        zc.append(cp)
    own = pltpu.make_async_copy(wcols(s), zbuf.at[z * 2 + s], ss.at[ZW])
    own.start()

    def grouped(row):
        rows = jnp.broadcast_to(row, (8, C))
        small = jnp.dot(rows, ind[...], precision=lax.Precision.HIGHEST, preferred_element_type=F32)
        return jnp.dot(small, indt[...], precision=lax.Precision.HIGHEST,
                       preferred_element_type=F32)[0:1] / ENTRIES

    def thirds(v):
        top = v.astype(BF16)
        rest = v - top.astype(F32)
        mid = rest.astype(BF16)
        return jnp.concatenate([top.astype(F32), mid.astype(F32), rest - mid.astype(F32)], axis=0).astype(BF16)

    def moved(v, side):
        parts = lax.dot_general(thirds(v), perm[...], (((1,), (side,)), ((), ())),
                                preferred_element_type=F32)
        return parts[0:8] + parts[8:16] + parts[16:24]

    bias = p_bias[...].reshape(1, C)
    row8 = lax.broadcasted_iota(jnp.int32, (8, C), 0)
    inner = moved(jnp.where(row8 == 0, p_gain[...].reshape(1, C), p_shift[...].reshape(1, C)), 0)
    gain, shift = inner[0:1], inner[1:2]
    xs[...] = jnp.dot(feat[...], perm[...], preferred_element_type=F32)
    mu = grouped(jnp.sum(xs[...], axis=0, keepdims=True))
    centred = xs[...] - mu
    xs[...] = centred
    inverse = lax.rsqrt(grouped(jnp.sum(centred * centred, axis=0, keepdims=True)) + EPS)
    xhat = xs[...] * inverse
    xs[...] = xhat
    pre = xhat * gain + shift
    sg = 1.0 / (1.0 + jnp.exp(-pre))
    ds[...] = sg * (1.0 + pre * (1.0 - sg))
    hid = pre * sg
    hb[...] = hid.astype(BF16)
    ht[:, 0:PIX] = hid.T.astype(BF16)
    def ring_gather(pos, right, left, piece, base):
        rt, lf = (pos + 1) % 4, (pos + 3) % 4
        first_sends = [
            rc(piece(pos, 0), piece(pos, 0), base, right),
            rc(piece(pos, 1), piece(pos, 1), base + 1, left),
            rc(piece(pos, 1), piece(pos, 1), base + 2, right),
            rc(piece(pos, 0), piece(pos, 0), base + 3, left),
        ]
        for cp in first_sends:
            cp.start()

        def relay(arrived):
            first_sends[0].wait_recv()
            f0 = rc(piece(lf, 0), piece(lf, 0), base + 4, right)
            f0.start()
            first_sends[1].wait_recv()
            f1 = rc(piece(rt, 1), piece(rt, 1), base + 5, left)
            f1.start()
            arrived(lf, 0, 1)
            arrived(rt, 1, 2)

            def sides():
                first_sends[2].wait_recv()
                arrived(lf, 1, 1)
                first_sends[3].wait_recv()
                arrived(rt, 0, 2)

            def finish():
                opp = (pos + 2) % 4
                f0.wait_recv()
                arrived(opp, 0, 3)
                f1.wait_recv()
                arrived(opp, 1, 3)
                for cp in first_sends + [f0, f1]:
                    cp.wait_send()
            return sides, finish
        return relay

    def piece_b(j, half):
        return wall.at[s * 16 + ra * 4 + j, pl.ds(half * 160, 160)]

    def piece_a(j, half):
        return wall.at[pl.ds(s * 16 + j * 4 + half * 2, 2)]


    sib_h = rc(ht.at[:, pl.ds(0, PIX)], ht.at[:, pl.ds(PIX, PIX)], SIB + 1, sib)
    sib_h.start()


    sib_c.wait_recv()
    windows(scot, PIX)
    sib_h.wait_recv()

    def chunk(sc, n, late):
        e = 1 - late
        l2 = (1 - sc) * (n % 2) + sc * ((lo + e) % 2)
        xx = (1 - sc) * ((x + e + 2 * (n // 2)) % 4) + sc * n
        return l2 * 4 + xx

    def wgrad(i):
        res = jnp.dot(ht[...], cc[s * 8 + i], preferred_element_type=F32).astype(BF16)
        l2, xx = i // 4, i % 4
        for hh in range(2):
            yy = hh * 2 + l2
            idx = (1 - s) * (xx * 4 + yy) + s * (yy * 4 + xx)
            term[idx] = res[hh * BLK:(hh + 1) * BLK]


    sib_w = {}

    def to_sibling(j, half, rel):
        cp = rc(piece_a(j, half), piece_a(j, half), SW + rel * 2 + half, sib)
        cp.start()
        sib_w[rel, half] = cp

    def ring_reduce(pos, right, left, piece, o, r, base, add, between=lambda: None):
        rt, lf, opp = (pos + 1) % 4, (pos + 3) % 4, (pos + 2) % 4
        sends = [
            rc(piece(opp, 0), o(0), base, right),
            rc(piece(opp, 1), o(1), base + 1, left),
            rc(piece(rt, 1), r(0, 1), base + 2, right),
            rc(piece(lf, 0), r(1, 0), base + 3, left),
        ]
        for cp in sends[:2]:
            cp.start()
        between()
        for cp in sends[2:]:
            cp.start()

        def middle():
            sends[0].wait_recv()
            add(rt, 0)
            g0 = rc(piece(rt, 0), r(0, 0), base + 4, right)
            g0.start()
            sends[1].wait_recv()
            add(lf, 1)
            g1 = rc(piece(lf, 1), r(1, 1), base + 5, left)
            g1.start()

            def finish():
                for cp in (sends[2], sends[3], g0, g1):
                    cp.wait_recv()
                for cp in sends + [g0, g1]:
                    cp.wait_send()
            return finish
        return middle

    def add_a(j, half):
        @pl.loop(0, 2)
        def _(q):
            at = j * 4 + half * 2 + q
            term[at] = (term[at].astype(F32) + o1[half * 2 + q].astype(F32)).astype(BF16)

    pl.loop(0, 4)(lambda n: wgrad(chunk(s, n, 1)))
    middle_ra = ring_reduce(
        ra, a_right, a_left,
        lambda j, half: term.at[pl.ds(j * 4 + half * 2, 2)],
        lambda half: o1.at[pl.ds(half * 2, 2)],
        lambda side, half: r1.at[side, pl.ds(half * 2, 2)],
        RSA, add_a, between=lambda: pl.loop(0, 4)(lambda n: wgrad(chunk(s, n, 0))))

    own.wait()
    for cp in zc:
        cp.wait_recv()
    for q in range(16):
        mf[q * 20:(q + 1) * 20, :] = zbuf[q].astype(F32)
    me = s * 16 + ra * 4 + rb
    wall[me] = mf[...].astype(BF16)

    relay_b = ring_gather(rb, b_right, b_left, piece_b, AGB)
    finish_ra = middle_ra()
    for step in relay_b(lambda j, half, rel: None):
        step()
    relay_a = ring_gather(ra, a_right, a_left, piece_a, AGA)
    to_sibling(ra, 0, 0)
    to_sibling(ra, 1, 0)

    finish_ra()

    def sum_a(j):
        return term[ra * 4 + j].astype(F32) + r1[0, j].astype(F32) + r1[1, j].astype(F32)

    @pl.loop(0, 4)
    def _(j):
        ub[j] = sum_a(j).astype(BF16)

    def add_b(j, half):
        part = pl.ds(half * 160, 160)
        ub[j, part] = (ub[j, part].astype(F32) + o2[half].astype(F32)).astype(BF16)

    middle_rb = ring_reduce(
        rb, b_right, b_left,
        lambda j, half: ub.at[j, pl.ds(half * 160, 160)],
        lambda half: o2.at[half],
        lambda side, half: r2.at[side, pl.ds(half * 160, 160)],
        RSB, add_b)
    sides_a, finish_a = relay_a(to_sibling)
    finish_rb = middle_rb()

    gh[...] = jnp.zeros((PIX, C), F32)

    def block(sc, i):
        l2, xx = i // 4, i % 4
        rows = []
        for hh in range(2):
            yy = hh * 2 + l2
            rows.append(wall[sc * 16 + (1 - sc) * (xx * 4 + yy) + sc * (yy * 4 + xx)])
        return jnp.concatenate(rows, axis=0)

    def back(sc, i):
        gh[...] += lax.dot_general(cc[sc * 8 + i, 0:PIX], block(sc, i), (((1,), (1,)), ((), ())),
                                   preferred_element_type=F32)

    def forth(sc, i):
        pbuf[sc * 8 + i] = jnp.dot(hb[...], block(sc, i), preferred_element_type=F32)

    def loop(f, sc, late):
        pl.loop(0, 4)(lambda n: f(sc, chunk(sc, n, late)))

    def both(sc, i):
        wk = block(sc, i)
        k = sc * 8 + i
        pbuf[k] = jnp.dot(hb[...], wk, preferred_element_type=F32)
        gh[...] += lax.dot_general(cc[k, 0:PIX], wk, (((1,), (1,)), ((), ())),
                                   preferred_element_type=F32)

    finish_rb()
    total = sum_a(rb) + r2[0].astype(F32) + r2[1].astype(F32)
    for q in range(NZ):
        tf[q] = total[q * 40:(q + 1) * 40]
        vb[q] = total[q * 40:(q + 1) * 40].astype(BF16)
    pc = []
    for dz in range(1, NZ):
        cp = rc(vb.at[(z + dz) % NZ], cr.at[z], PC + dz, dev(x, y, (z + dz) % NZ, s))
        cp.start()
        pc.append(cp)
    cr[z] = jnp.zeros((40, CH), BF16)

    sides_a()
    loop(both, s, 0)

    for cp in pc:
        cp.wait_recv()
    full = (jnp.sum(cr[...].astype(F32), axis=0) + tf[z]) / IMAGES
    f2[0] = full[0:20]
    f2[1] = full[20:40]
    slot = s * 8 + lo * 4 + x
    rf[slot] = f2[s]
    fc = []
    for dl, dx, dc in fpeers:
        cp = rc(f2.at[(s + dc) % 2], rf.at[slot], FIN + dl * 8 + dx * 2 + dc, fdev(dl, dx, dc))
        cp.start()
        fc.append(cp)

    for rel, half in ((1, 0), (2, 1), (1, 1), (2, 0)):
        sib_w[rel, half].wait_recv()
    loop(both, 1 - s, 0)
    finish_a()
    loop(back, s, 1)
    for rel, half in ((0, 0), (0, 1), (3, 0), (3, 1)):
        sib_w[rel, half].wait_recv()
    loop(back, 1 - s, 1)

    gp = gh[...] * ds[...]
    gh[...] = gp
    shift_sum = jnp.sum(gp, axis=0, keepdims=True)
    gain_sum = jnp.sum(gp * xs[...], axis=0, keepdims=True)
    for i in range(5):
        vs[0, i:i + 1, :] = gain_sum[:, i * 128:(i + 1) * 128]
        vs[0, 5 + i:6 + i, :] = shift_sum[:, i * 128:(i + 1) * 128]
    v1[z * 2 + s] = vs[0]
    vc = []
    for dz, dc in zpeers:
        cp = rc(vs.at[0], v1.at[z * 2 + s], V1 + dz * 2 + dc, zdev(dz, dc))
        cp.start()
        vc.append(cp)

    m1 = grouped(shift_sum * gain)
    m2 = grouped(gain_sum * gain)
    g = gh[...] * gain
    fgp = ((g - m1 - xs[...] * m2) * inverse).astype(BF16)
    fg[...] = lax.dot_general(fgp, perm[...], (((1,), (1,)), ((), ())),
                              preferred_element_type=F32).astype(BF16)

    for cp in vc:
        cp.wait_recv()
    vs[1] = jnp.sum(v1[...], axis=0)
    v2[x] = vs[1]
    vx = []
    for k in (1, 2, 3):
        cp = rc(vs.at[1], v2.at[x], V2 + k, dev((x + k) % 4, y, z, s))
        cp.start()
        vx.append(cp)
    loop(forth, s, 1)
    for cp in vx:
        cp.wait_recv()
    vs[2] = jnp.sum(v2[...], axis=0)
    v3[y] = vs[2]
    vy = []
    for k in (1, 2, 3):
        cp = rc(vs.at[2], v3.at[y], V3 + k, dev(x, (y + k) % 4, z, s))
        cp.start()
        vy.append(cp)
    loop(forth, 1 - s, 1)

    for ot in range(5):
        total = None
        for b in range(3):
            parts = []
            for a in range(3):
                k, i = divmod(5 * (3 * a + b) + ot, 3)
                p = pbuf[k, :, i * 128:(i + 1) * 128]
                pad = jnp.zeros((SIDE, 128), F32)
                if a == 0:
                    p = jnp.concatenate([pad, p[:PIX - SIDE]], axis=0)
                elif a == 2:
                    p = jnp.concatenate([p[SIDE:], pad], axis=0)
                parts.append(p)
            sb = parts[0] + parts[1] + parts[2]
            if b == 0:
                sb = jnp.where(first[:, :128], 0.0, pltpu.roll(sb, 1, 0))
            elif b == 2:
                sb = jnp.where(last[:, :128], 0.0, pltpu.roll(sb, PIX - 1, 0))
            total = sb if total is None else total + sb
        cols = slice(ot * 128, (ot + 1) * 128)
        out[:, cols] = (total + bias[:, cols]).astype(BF16)

    for cp in fc:
        cp.wait_recv()
    for k in range(15):
        wg[:, k * CH:(k + 1) * CH] = rf[k]
    for cp in vy:
        cp.wait_recv()
    sums = jnp.sum(v3[...], axis=0) / IMAGES
    vo[...] = jnp.zeros((8, C), F32)
    for q in range(3):
        for i in range(5):
            vo[q:q + 1, i * 128:(i + 1) * 128] = sums[q * 5 + i:q * 5 + i + 1]
    outer = moved(vo[...], 1)
    out_gain[...] = outer[0:1].reshape(C)
    out_shift[...] = outer[1:2].reshape(C)
    out_bias[...] = vo[2:3].reshape(C)
    for cp in zc + [sib_c, sib_h] + list(sib_w.values()) + vc + vx + vy + pc + fc:
        cp.wait_send()


def local(features, weight, gain, shift, bias, cotangent):
    order = np.arange(C).reshape(NZ, 2, GROUP).transpose(1, 0, 2).reshape(C)
    perm = np.zeros((C, C), np.float32)
    perm[order, np.arange(C)] = 1.0
    ind = np.zeros((C, 128), np.float32)
    ind[np.arange(C), np.arange(C) // GROUP] = 1.0
    vm = pl.BlockSpec(memory_space=pltpu.VMEM)
    out, fg, wg, g_gain, g_shift, g_bias = pl.pallas_call(
        kernel,
        name="fused_step",
        out_shape=[
            jax.ShapeDtypeStruct((PIX, C), BF16),
            jax.ShapeDtypeStruct((PIX, C), BF16),
            jax.ShapeDtypeStruct((20, 9 * C), F32),
            jax.ShapeDtypeStruct((C,), F32),
            jax.ShapeDtypeStruct((C,), F32),
            jax.ShapeDtypeStruct((C,), F32),
        ],
        in_specs=[vm] * 9,
        out_specs=[vm] * 6,
        scratch_shapes=[
            pltpu.VMEM((16, 20, CH), BF16),
            pltpu.VMEM((BLK, CH), F32),
            pltpu.VMEM((32, BLK, CH), BF16),
            pltpu.VMEM((16, BLK, CH), BF16),
            pltpu.VMEM((PIX, C), F32),
            pltpu.VMEM((PIX, C), F32),
            pltpu.VMEM((PIX, C), BF16),
            pltpu.VMEM((C, 2 * PIX), BF16),
            pltpu.VMEM((16, 2 * PIX, CH), BF16),
            pltpu.VMEM((3, PIX + 2 * SIDE, C), BF16),
            pltpu.VMEM((16, PIX, CH), F32),
            pltpu.VMEM((PIX, C), F32),
            pltpu.VMEM((4, BLK, CH), BF16),
            pltpu.VMEM((2, 4, BLK, CH), BF16),
            pltpu.VMEM((4, BLK, CH), BF16),
            pltpu.VMEM((2, 160, CH), BF16),
            pltpu.VMEM((2, BLK, CH), BF16),
            pltpu.VMEM((NZ, 40, CH), BF16),
            pltpu.VMEM((NZ, 40, CH), BF16),
            pltpu.VMEM((NZ, 40, CH), F32),
            pltpu.VMEM((2, 20, CH), F32),
            pltpu.VMEM((16, 20, CH), F32),
            pltpu.VMEM((3, 16, 128), F32),
            pltpu.VMEM((16, 16, 128), F32),
            pltpu.VMEM((4, 16, 128), F32),
            pltpu.VMEM((4, 16, 128), F32),
            pltpu.VMEM((PIX, C), BF16),
            pltpu.VMEM((8, C), F32),
            pltpu.SemaphoreType.DMA((NSEM,)),
            pltpu.SemaphoreType.DMA((NSEM,)),
        ],
        compiler_params=pltpu.CompilerParams(
            collective_id=0, has_side_effects=True, vmem_limit_bytes=60 * 1024 * 1024),
    )(features.reshape(PIX, C), weight, gain, shift, bias, cotangent.reshape(PIX, C),
      jnp.asarray(perm, BF16), jnp.asarray(ind), jnp.asarray(ind.T.copy()))
    shape = features.shape
    return out.reshape(shape), fg.reshape(shape), wg, g_gain, g_shift, g_bias


def solution(mesh):
    img = P(("fsdp", "dp"), None, None, None)
    return jax.shard_map(
        local, mesh=mesh,
        in_specs=(img, P("fsdp", None), P(), P(), P(), img),
        out_specs=(img, img, P("fsdp", None), P(), P(), P()),
        check_vma=False)
```

time: 111 us -> 88.5 us (0.80)
  Pallas kernels: 100 us -> 81 us
  local copies, waits for them, and re-layouts: 8.6 us -> 5.28 us
    pallas_call x1, Pallas kernels: 100 us -> 81 us  [local(): pl.pallas_call(kernel, name='fused_step', out_shape=[jax.ShapeDtypeStruct...]
    another operation x8 -> x0, local copies, waits for them, and re-layouts: 1.69 us -> none  [the longest x4 1.52 us: local(): par = jnp.stack([to_inner(gain), to_inner(shift), bias] + [bias] * 5)]
    reshape x4 -> x0, local copies, waits for them, and re-layouts: 1.54 us -> none  [the longest x2 1.36 us: to_outer(): return v.reshape(2, NZ, GROUP).transpose(1, 0, 2).reshape(C)]
    slice x1 -> x0, local copies, waits for them, and re-layouts: 1.45 us -> none  [local(): vec[2]]
    unnamed x11 -> x16, local copies, waits for them, and re-layouts: 3.92 us -> 5.28 us
where the time goes in v3:
time: 88.5 us; the launch traced here: 87 us
  Pallas kernels  81 us (92%)
  local copies, waits for them, and re-layouts  5.28 us (6%)
    pallas_call x1, Pallas kernels, local(): pl.pallas_call(kernel, name='fused_step', out_shape=[jax.ShapeDtypeStruct...  81 us
    unnamed x16, local copies, waits for them, and re-layouts  5.28 us

profile of v3, /device:TPU:64, one launch (start us, length us, event | category | flops | bytes accessed | tf_op | source)
XLA Modules:
  0.0 87.0 jit_solution(12740296943811732318)
XLA Ops:
  0.6 81.0 %fused_step.1 = (bf16[256,640]{1,0:T(8,128)(2,1)}, bf16[256,640]{1,0:T(8,128)(2,1)}, f32[20,5760]{1,0:T(8,128)}, f32[640]{0:T(1024)}, f32[640]{0:T(1024)}, /*index=5*/f32[640]{0:T(1024)}) custom-call(bf16[256,640]{1,0:T(8,128)(2,1)} %bitcast.6, bf16[20,5760]{1,0:T(8,128)(2,1)} %w.1, f32[640]{0:T(1024)} %p_gain.1, f32[640]{0:T(1024)} %p_shift.1, f32[640]{0:T(1024)} %p_bias.1, ...), custom_call_target="tpu_custom_call" | custom-call | tf_op jit(solution)/shard_map/fused_step/pallas_call | solution.py:460
  81.7 0.0 copy-start.1
  81.7 0.0 copy-start
  81.7 1.8 %copy.21 = bf16[1,16,16,640]{3,2,1,0:T(8,128)(2,1)} copy(bf16[1,16,16,640]{3,2,1,0:T(8,128)(2,1)} %bitcast.5) | data formatting | bytes 655360
  83.5 0.0 copy-done.1
  83.5 0.7 copy.22
  84.2 0.0 copy-done
  84.2 0.0 copy-start.4
  84.2 0.8 copy.23
  85.0 0.0 copy-done.4
  85.0 0.0 copy-start.3
  85.1 0.6 copy.24
  85.6 0.1 copy-done.3
  85.7 0.0 copy-start.2
  85.7 0.6 copy.25
  86.3 0.1 copy-done.2
  86.4 0.6 copy.26
Async XLA Ops:
  81.7 1.8 %copy-start.1 = (bf16[256,640]{1,0:T(8,128)(2,1)S(1)}, bf16[256,640]{1,0:T(8,128)(2,1)}, u32[]{:S(2)}) copy-start(bf16[256,640]{1,0:T(8,128)(2,1)} %get-tuple-element.13) | copy-start | bytes 983044
  81.7 2.5 %copy-start = (f32[20,5760]{1,0:T(8,128)S(1)}, f32[20,5760]{1,0:T(8,128)}, u32[]{:S(2)}) copy-start(f32[20,5760]{1,0:T(8,128)} %get-tuple-element.26) | copy-start | bytes 1382404
  84.2 0.8 copy-start.4
  85.0 0.7 copy-start.3
  85.7 0.7 copy-start.2

commit v4 on v3

--- a/solution.py
+++ b/solution.py
@@ -26,10 +26,11 @@
     0, 16, 22, 28, 34, 40, 42, 50, 58, 74, 90, 94, 98)
 
 
-def kernel(feat, w, p_gain, p_shift, p_bias, cot, perm, ind, indt,
+def kernel(feat_in, w_in, p_gain_in, p_shift_in, p_bias_in, cot_in, perm_in, ind_in, indt_in,
            out, fg, wg, out_gain, out_shift, out_bias,
            zbuf, mf, wall, term, xs, ds, hb, ht, cc, cb, pbuf, gh,
-           o1, r1, ub, o2, r2, vb, cr, tf, f2, rf, vs, v1, v2, v3, scot, vo, ss, rs):
+           o1, r1, ub, o2, r2, vb, cr, tf, f2, rf, vs, v1, v2, v3, scot, vo,
+           feat, w, p_gain, p_shift, p_bias, cot, perm, ind, indt, ls, ss, rs):
     fi = lax.axis_index("fsdp")
     di = lax.axis_index("dp")
     z = fi // 4
@@ -69,6 +70,12 @@
     everyone += [dev(x, (y + k) % 4, z, s) for k in (1, 2, 3)]
     for device in everyone:
         pl.semaphore_signal(barrier, inc=1, device_id=device, device_id_type=MESH)
+
+    pairs = [(cot_in, cot), (feat_in, feat), (perm_in, perm), (ind_in, ind), (indt_in, indt),
+             (w_in, w), (p_gain_in, p_gain), (p_shift_in, p_shift), (p_bias_in, p_bias)]
+    loads = [pltpu.make_async_copy(a, b, ls.at[i]) for i, (a, b) in enumerate(pairs)]
+    for cp in loads:
+        cp.start()
 
     pj = lax.broadcasted_iota(jnp.int32, (PIX, C), 0) % SIDE
     first, last = pj == 0, pj == SIDE - 1
@@ -91,25 +98,11 @@
         cc[15, at:at + PIX, :] = jnp.zeros((PIX, CH), BF16)
         return jnp.sum(wide, axis=0, keepdims=True)
 
+    loads[0].wait()
     bias_sum = windows(cot, 0)
     for i in range(5):
         vs[0, 10 + i:11 + i, :] = bias_sum[:, i * 128:(i + 1) * 128]
     vs[0, 15:16, :] = jnp.zeros((1, 128), F32)
-    pl.semaphore_wait(barrier, len(everyone))
-    sib_c = rc(cot, scot, SIB, sib)
-    sib_c.start()
-    def wcols(sc):
-        k = jnp.minimum(sc * 8 + lo * 4 + x, 14)
-        return w.at[:, pl.ds(pl.multiple_of(k * CH, CH), CH)]
-
-    zc = []
-    for dz, dc in zpeers:
-        cp = rc(wcols((s + dc) % 2), zbuf.at[z * 2 + s], ZW + dz * 2 + dc, zdev(dz, dc))
-        cp.start()
-        zc.append(cp)
-    own = pltpu.make_async_copy(wcols(s), zbuf.at[z * 2 + s], ss.at[ZW])
-    own.start()
-
     def grouped(row):
         rows = jnp.broadcast_to(row, (8, C))
         small = jnp.dot(rows, ind[...], precision=lax.Precision.HIGHEST, preferred_element_type=F32)
@@ -127,6 +120,8 @@
                                 preferred_element_type=F32)
         return parts[0:8] + parts[8:16] + parts[16:24]
 
+    for cp in loads[1:]:
+        cp.wait()
     bias = p_bias[...].reshape(1, C)
     row8 = lax.broadcasted_iota(jnp.int32, (8, C), 0)
     inner = moved(jnp.where(row8 == 0, p_gain[...].reshape(1, C), p_shift[...].reshape(1, C)), 0)
@@ -136,6 +131,22 @@
     centred = xs[...] - mu
     xs[...] = centred
     inverse = lax.rsqrt(grouped(jnp.sum(centred * centred, axis=0, keepdims=True)) + EPS)
+
+    pl.semaphore_wait(barrier, len(everyone))
+    sib_c = rc(cot, scot, SIB, sib)
+    sib_c.start()
+    def wcols(sc):
+        k = jnp.minimum(sc * 8 + lo * 4 + x, 14)
+        return w.at[:, pl.ds(pl.multiple_of(k * CH, CH), CH)]
+
+    zc = []
+    for dz, dc in zpeers:
+        cp = rc(wcols((s + dc) % 2), zbuf.at[z * 2 + s], ZW + dz * 2 + dc, zdev(dz, dc))
+        cp.start()
+        zc.append(cp)
+    own = pltpu.make_async_copy(wcols(s), zbuf.at[z * 2 + s], ss.at[ZW])
+    own.start()
+
     xhat = xs[...] * inverse
     xs[...] = xhat
     pre = xhat * gain + shift
@@ -450,6 +461,15 @@
         cp.wait_send()
 
 
+def put_out(*refs):
+    sems = refs[12]
+    copies = [pltpu.make_async_copy(refs[i], refs[6 + i], sems.at[i]) for i in range(6)]
+    for cp in copies:
+        cp.start()
+    for cp in copies:
+        cp.wait()
+
+
 def local(features, weight, gain, shift, bias, cotangent):
     order = np.arange(C).reshape(NZ, 2, GROUP).transpose(1, 0, 2).reshape(C)
     perm = np.zeros((C, C), np.float32)
@@ -457,18 +477,18 @@
     ind = np.zeros((C, 128), np.float32)
     ind[np.arange(C), np.arange(C) // GROUP] = 1.0
     vm = pl.BlockSpec(memory_space=pltpu.VMEM)
-    out, fg, wg, g_gain, g_shift, g_bias = pl.pallas_call(
+    held = pl.pallas_call(
         kernel,
         name="fused_step",
         out_shape=[
-            jax.ShapeDtypeStruct((PIX, C), BF16),
-            jax.ShapeDtypeStruct((PIX, C), BF16),
-            jax.ShapeDtypeStruct((20, 9 * C), F32),
-            jax.ShapeDtypeStruct((C,), F32),
-            jax.ShapeDtypeStruct((C,), F32),
-            jax.ShapeDtypeStruct((C,), F32),
+            pltpu.VMEM((PIX, C), BF16),
+            pltpu.VMEM((PIX, C), BF16),
+            pltpu.VMEM((20, 9 * C), F32),
+            pltpu.VMEM((C,), F32),
+            pltpu.VMEM((C,), F32),
+            pltpu.VMEM((C,), F32),
         ],
-        in_specs=[vm] * 9,
+        in_specs=[pl.BlockSpec(memory_space=pl.ANY)] * 9,
         out_specs=[vm] * 6,
         scratch_shapes=[
             pltpu.VMEM((16, 20, CH), BF16),
@@ -499,6 +519,16 @@
             pltpu.VMEM((4, 16, 128), F32),
             pltpu.VMEM((PIX, C), BF16),
             pltpu.VMEM((8, C), F32),
+            pltpu.VMEM((PIX, C), BF16),
+            pltpu.VMEM((20, 9 * C), BF16),
+            pltpu.VMEM((C,), F32),
+            pltpu.VMEM((C,), F32),
+            pltpu.VMEM((C,), F32),
+            pltpu.VMEM((PIX, C), BF16),
+            pltpu.VMEM((C, C), BF16),
+            pltpu.VMEM((C, 128), F32),
+            pltpu.VMEM((128, C), F32),
+            pltpu.SemaphoreType.DMA((9,)),
             pltpu.SemaphoreType.DMA((NSEM,)),
             pltpu.SemaphoreType.DMA((NSEM,)),
         ],
@@ -507,6 +537,15 @@
     )(features.reshape(PIX, C), weight, gain, shift, bias, cotangent.reshape(PIX, C),
       jnp.asarray(perm, BF16), jnp.asarray(ind), jnp.asarray(ind.T.copy()))
     shape = features.shape
+    out, fg, wg, g_gain, g_shift, g_bias = pl.pallas_call(
+        put_out,
+        name="put_out",
+        out_shape=[jax.ShapeDtypeStruct(v.shape, v.dtype) for v in held],
+        in_specs=[vm] * 6,
+        out_specs=[pl.BlockSpec(memory_space=pl.ANY)] * 6,
+        scratch_shapes=[pltpu.SemaphoreType.DMA((6,))],
+        compiler_params=pltpu.CompilerParams(vmem_limit_bytes=8 * 1024 * 1024),
+    )(*held)
     return out.reshape(shape), fg.reshape(shape), wg, g_gain, g_shift, g_bias
 
 

time: 88.5 us -> 80.8 us (0.913); the launches traced: 87 us -> 80.5 us
  local copies, waits for them, and re-layouts: 5.28 us -> 0 us
  Pallas kernels: 81 us -> 79.9 us
    unnamed x16 -> x0, local copies, waits for them, and re-layouts: 5.28 us -> none
    pallas_call x1 -> x2, Pallas kernels: 81 us -> 79.9 us  [the longest x1 78.8 us: local(): pl.pallas_call(kernel, name='fused_step', out_shape=[pltpu.VMEM((PIX, C),...]
where the time goes in v4:
time: 80.8 us; the launch traced here: 80.5 us
  Pallas kernels  79.9 us (99%)
    pallas_call x1, Pallas kernels, local(): pl.pallas_call(kernel, name='fused_step', out_shape=[pltpu.VMEM((PIX, C),...  78.8 us

profile of v4, /device:TPU:64, one launch (start us, length us, event | category | flops | bytes accessed | tf_op | source)
XLA Modules:
  0.0 80.5 jit_solution(4398538638063975652)
XLA Ops:
  0.6 78.8 %fused_step.1 = (bf16[256,640]{1,0:T(8,128)(2,1)S(1)}, bf16[256,640]{1,0:T(8,128)(2,1)S(1)}, f32[20,5760]{1,0:T(8,128)S(1)}, f32[640]{0:T(1024)S(1)}, f32[640]{0:T(1024)S(1)}, /*index=5*/f32[640]{0:T(1024)S(1)}) custom-call(bf16[256,640]{1,0:T(8,128)(2,1)} %bitcast.4, bf16[20,5760]{1,0:T(8,128)(2,1)} %w_in.1, f32[640]{0:T(1024)} %p_gain_in.1, ...), custom_call_target="tpu_custom_call" | custom-call | tf_op jit(solution)/shard_map/fused_step/pallas_call | solution.py:480
  79.5 1.1 %put_out.1 = (bf16[256,640]{1,0:T(8,128)(2,1)}, bf16[256,640]{1,0:T(8,128)(2,1)}, f32[20,5760]{1,0:T(8,128)}, f32[640]{0:T(1024)}, f32[640]{0:T(1024)}, /*index=5*/f32[640]{0:T(1024)}) custom-call(bf16[256,640]{1,0:T(8,128)(2,1)S(1)} %get-tuple-element.18.refs_0_, bf16[256,640]{1,0:T(8,128)(2,1)S(1)} %get-tuple-element.19.refs_1_, ...), custom_call_target="tpu_custom_call" | custom-call | tf_op jit(solution)/shard_map/put_out/pallas_call | solution.py:540
